TPU v7x, 32 devices: a whole 2x2x4 slice. The times are simulated.
32 devices in a mesh: grp: 2 (over y), ctx: 4 (over z), head: 2 (over x), sub: 2 (over core).
Axes of the slice: x: 2, y: 2, z: 4, core: 2. Of those that a mesh axis runs over, the one named last changes fastest.
Arguments:
- queries: bfloat16 [1024, 8192], P(('grp', 'ctx'), 'head'), parts along dimension 0, may hold values from -120 to 120
- stretch_keys: bfloat16 [1024, 1024], P(('grp', 'ctx', 'sub'), 'head'), parts along dimension 0, may hold values from -6 to 6
- stretch_values: bfloat16 [1024, 1024], P(('grp', 'ctx', 'sub'), 'head'), parts along dimension 0, may hold values from -6 to 6
- cache_keys: bfloat16 [3072, 1024], P(('grp', 'ctx', 'sub'), 'head'), parts along dimension 0, may hold values from -6 to 6
- cache_values: bfloat16 [3072, 1024], P(('grp', 'ctx', 'sub'), 'head'), parts along dimension 0, may hold values from -6 to 6
- doc_lengths: int32 [24], P('grp'), parts along dimension 0, may hold values from 1 to 256, 2048 in all
Outputs:
- attended: bfloat16 [1024, 8192], P(('grp', 'ctx'), ('head', 'sub')), parts along dimension 0
There are 2 independent parts, one for each index of `grp`. A program takes and returns all parts, laid end to end along the dimension named above; each array names one. Nothing has to cross between parts.
Inputs may be any that keep to these rules, and one draw needn't show every extreme that they name: `doc_lengths`: the 12 documents fill all 2048 positions in order, none longer than 256 tokens and one exactly 256.
All inputs are finite; a program needn't handle non-finite values.
Results may differ from a plain program's by a relative error of at most 0.013.
Values may be sent and summed in bfloat16 or wider, within the bound.
A program may use at most 64 MiB of HBM per device.

v0:
```python
import functools

import jax
import jax.numpy as jnp
from jax import lax
from jax.experimental import pallas as pl
from jax.experimental.pallas import tpu as pltpu
from jax.sharding import PartitionSpec as P

HEAD_DIM = 128
NEG_FILL = -1e30
LOG2_E = 1.4426950408889634


def kernel(
    n_ctx,
    n_sub,
    q_hbm,
    sk_hbm,
    sv_hbm,
    ck_hbm,
    cv_hbm,
    docs_hbm,
    out_ref,
    q_v,
    k_buf,
    v_buf,
    docs,
    max_v,
    sum_v,
    acc_v,
    part_v,
    q_sem,
    docs_sem,
    own_sem,
    pair_send,
    next_send,
    cache_send,
    relay_send,
    recv_sem,
    turn_sem,
):
    ctx = lax.axis_index("ctx")
    sub = lax.axis_index("sub")
    flat = ctx * n_sub + sub
    rows = q_hbm.shape[0]
    unit = sk_hbm.shape[0]
    all_groups = sk_hbm.shape[1] // HEAD_DIM
    groups = max(1, all_groups // n_sub)
    cols = groups * HEAD_DIM
    heads = q_hbm.shape[1] // HEAD_DIM // n_sub
    per_group = heads // groups
    per_cache = ck_hbm.shape[0] // unit
    prefix_units = per_cache * n_sub * n_ctx
    reach = n_ctx // 2
    back = reach * n_sub
    ndoc = docs_hbm.shape[0]
    scale = HEAD_DIM**-0.5 * LOG2_E

    def remote(src, dst, send, recv, to_ctx, to_sub):
        return pltpu.make_async_remote_copy(
            src_ref=src,
            dst_ref=dst,
            send_sem=send,
            recv_sem=recv,
            device_id={"ctx": to_ctx, "sub": to_sub},
            device_id_type=pl.DeviceIdType.MESH,
        )

    def slot(buf, k):
        start = k * unit
        if not isinstance(k, int):
            start = pl.multiple_of(start, unit)
        return buf.at[pl.ds(start, unit), :]

    def columns(to_sub):
        start = to_sub * all_groups // n_sub * HEAD_DIM
        if not isinstance(start, int):
            start = pl.multiple_of(start, HEAD_DIM)
        return pl.ds(start, cols)

    bufs = (k_buf, v_buf)
    stretch = (sk_hbm, sv_hbm)
    cache = (ck_hbm, cv_hbm)

    barrier = pltpu.get_barrier_semaphore()

    def greet(to_ctx, to_sub):
        pl.semaphore_signal(
            barrier,
            inc=1,
            device_id={"ctx": to_ctx, "sub": to_sub},
            device_id_type=pl.DeviceIdType.MESH,
        )

    @pl.when(ctx == 0)
    def _():
        for k in range(back):
            source = (prefix_units - back + k) // per_cache
            greet(source // n_sub, source % n_sub)

    @pl.when(ctx >= 1)
    def _():
        for t in range(n_sub):
            greet(ctx - 1, t)

    for other in range(1, n_sub):
        greet(ctx, (sub + other) % n_sub)

    docs_copy = pltpu.make_async_copy(docs_hbm, docs, docs_sem)
    docs_copy.start()
    q_copies = []
    for h in range(heads):
        at = pl.multiple_of((sub * heads + h) * HEAD_DIM, HEAD_DIM)
        copy = pltpu.make_async_copy(
            q_hbm.at[:, pl.ds(at, HEAD_DIM)],
            q_v.at[pl.ds(h * rows, rows), :],
            q_sem.at[h],
        )
        copy.start()
        q_copies.append(copy)
    own_copies = []
    for i in range(2):
        copy = pltpu.make_async_copy(
            stretch[i].at[:, columns(sub)],
            slot(bufs[i], back + sub),
            own_sem.at[i],
        )
        copy.start()
        own_copies.append(copy)

    def offset(j):
        return flat * per_cache + j - (prefix_units - back)

    expected = n_sub - 1 + jnp.where(ctx + 1 < n_ctx, n_sub, 0)
    for j in range(per_cache):
        expected = expected + jnp.where(offset(j) >= 0, n_sub, 0)
    pl.semaphore_wait(barrier, expected)

    def cache_copies(j, subs=range(n_sub)):
        to_slot = offset(j)
        copies = []
        for i in range(2):
            for t in subs:
                copies.append(
                    remote(
                        cache[i].at[pl.ds(j * unit, unit), columns(t)],
                        slot(bufs[i], to_slot),
                        cache_send.at[j, t, i],
                        recv_sem.at[to_slot, i],
                        0,
                        t,
                    )
                )
        return copies

    def next_copies():
        copies = []
        for t in range(n_sub):
            for i in range(2):
                to_slot = back - n_sub + sub
                copies.append(
                    remote(
                        stretch[i].at[:, columns(t)],
                        slot(bufs[i], to_slot),
                        next_send.at[t, i],
                        recv_sem.at[to_slot, i],
                        ctx + 1,
                        t,
                    )
                )
        return copies

    def pair_copies():
        copies = []
        for other in range(1, n_sub):
            to_sub = (sub + other) % n_sub
            for i in range(2):
                copies.append(
                    remote(
                        stretch[i].at[:, columns(to_sub)],
                        slot(bufs[i], back + sub),
                        pair_send.at[other - 1, i],
                        recv_sem.at[back + sub, i],
                        ctx,
                        to_sub,
                    )
                )
        return copies

    lowest = (prefix_units - back) // per_cache
    holder = (prefix_units - back + n_sub) // per_cache
    gated = lowest != holder and lowest // n_sub == holder // n_sub

    for j in reversed(range(per_cache)):

        @pl.when(offset(j) >= int(gated))
        def _(j=j):
            for copy in cache_copies(j):
                copy.start()

    @pl.when(ctx + 1 < n_ctx)
    def _():
        for copy in next_copies():
            copy.start()

    for copy in pair_copies():
        copy.start()

    half = n_sub // 2
    if gated:
        for j in range(per_cache):

            @pl.when(offset(j) == n_sub)
            def _(j=j):
                for copy in cache_copies(j, range(half)):
                    copy.wait_send()
                pl.semaphore_signal(
                    turn_sem,
                    inc=1,
                    device_id={"ctx": ctx, "sub": lowest % n_sub},
                    device_id_type=pl.DeviceIdType.MESH,
                )

        for j in range(per_cache):

            @pl.when(offset(j) == 0)
            def _(j=j):
                pl.semaphore_wait(turn_sem, 1)
                for copy in cache_copies(j):
                    copy.start()

    def relays(k, i, act):
        if k >= n_sub:

            @pl.when(ctx + 1 < n_ctx)
            def _():
                act(
                    remote(
                        slot(bufs[i], k),
                        slot(bufs[i], k - n_sub),
                        relay_send.at[k, i],
                        recv_sem.at[k - n_sub, i],
                        ctx + 1,
                        sub,
                    )
                )

    def arrived(k, i):
        piece = slot(bufs[i], k)
        remote(piece, piece, relay_send.at[0, i], recv_sem.at[k, i], ctx, sub).wait_recv()

    docs_copy.wait()
    q_pos = rows * ctx + prefix_units * unit + lax.broadcasted_iota(jnp.int32, (1, rows), 1)
    end = jnp.int32(0)
    first = jnp.zeros((1, rows), jnp.int32)
    for e in range(ndoc):
        end = end + docs[e]
        first = jnp.maximum(first, jnp.where(q_pos >= end, end, 0))

    wide = min(2, per_group)
    span = wide * rows

    def attend(distance):
        base = (reach - distance) * rows
        k_pos = (
            rows * (ctx - distance)
            + prefix_units * unit
            + lax.broadcasted_iota(jnp.int32, (rows, rows), 0)
        )
        allowed = k_pos >= first
        if distance == 0:
            allowed = allowed & (k_pos <= q_pos)
        bias = jnp.where(allowed, 0.0, NEG_FILL)
        bias = jnp.concatenate([bias] * wide, axis=1)
        blocks = [
            (g, (g * per_group + b * wide) * rows)
            for g in range(groups)
            for b in range(per_group // wide)
        ]

        def weigh(g, at):
            here = pl.ds(at, span)
            keys = k_buf[pl.ds(base, rows), pl.ds(g * HEAD_DIM, HEAD_DIM)]
            scores = lax.dot_general(
                keys,
                q_v[here, :],
                (((1,), (1,)), ((), ())),
                preferred_element_type=jnp.float32,
            )
            scores = scores + bias
            top = jnp.max(scores, axis=0, keepdims=True)
            if distance > 0:
                before = max_v[:, here]
                top = jnp.maximum(top, before)
            weights = jnp.exp2((scores - top) * scale)
            total = jnp.sum(weights, axis=0, keepdims=True)
            shrink = None
            if distance > 0:
                shrink = jnp.exp2((before - top) * scale)
                total = total + sum_v[:, here] * shrink
            if distance < reach:
                max_v[:, here] = top
            return weights.astype(jnp.bfloat16), total, shrink

        def add(g, at, weights, total, shrink):
            here = pl.ds(at, span)
            values = v_buf[pl.ds(base, rows), pl.ds(g * HEAD_DIM, HEAD_DIM)]
            update = lax.dot_general(
                values,
                weights,
                (((0,), (0,)), ((), ())),
                preferred_element_type=jnp.float32,
            )
            if 0 < distance < reach:
                update = update + acc_v[:, here] * shrink
            if distance < reach:
                sum_v[:, here] = total
                acc_v[:, here] = update
            else:
                result = (acc_v[:, here] + update * total).astype(out_ref.dtype)
                for w in range(wide):
                    piece = result[:, w * rows : (w + 1) * rows]
                    out_at = (at // rows + w) * HEAD_DIM
                    out_ref[:, pl.ds(out_at, HEAD_DIM)] = piece.T

        if distance < reach:
            for g, at in blocks:
                add(g, at, *weigh(g, at))
            return
        take(distance, (0,))
        for g, at in blocks:
            weights, total, shrink = weigh(g, at)
            here = pl.ds(at, span)
            part_v[:, here] = weights
            inverse = 1.0 / total
            sum_v[:, here] = inverse
            acc_v[:, here] = acc_v[:, here] * (shrink * inverse)
        take(distance, (1,))
        for g, at in blocks:
            here = pl.ds(at, span)
            add(g, at, part_v[:, here], sum_v[:, here], None)

    for copy in own_copies:
        copy.wait()
    for copy in q_copies:
        copy.wait()
    for r in range(n_sub):

        @pl.when(sub != r)
        def _(r=r):
            for i in range(2):
                arrived(back + r, i)

    attend(0)

    def take(distance, kinds=(0, 1)):
        for r in reversed(range(n_sub)):
            k = back - distance * n_sub + r
            for i in kinds:
                arrived(k, i)
                relays(k, i, lambda copy: copy.start())

    for distance in range(1, reach + 1):
        if distance < reach:
            take(distance)
        attend(distance)

    for j in range(per_cache):

        @pl.when(offset(j) >= 0)
        def _(j=j):
            if gated:

                @pl.when(offset(j) != n_sub)
                def _():
                    for copy in cache_copies(j, range(half)):
                        copy.wait_send()

                for copy in cache_copies(j, range(half, n_sub)):
                    copy.wait_send()
            else:
                for copy in cache_copies(j):
                    copy.wait_send()

    @pl.when(ctx + 1 < n_ctx)
    def _():
        for copy in next_copies():
            copy.wait_send()

    for copy in pair_copies():
        copy.wait_send()
    for k in range(back):
        for i in range(2):
            relays(k, i, lambda copy: copy.wait_send())


def on_device(queries, stretch_keys, stretch_values, cache_keys, cache_values, doc_lengths):
    n_ctx = lax.axis_size("ctx")
    n_sub = lax.axis_size("sub")
    rows = queries.shape[0]
    unit = stretch_keys.shape[0]
    cols = max(1, stretch_keys.shape[1] // HEAD_DIM // n_sub) * HEAD_DIM
    per_cache = cache_keys.shape[0] // unit
    heads = queries.shape[1] // n_sub // HEAD_DIM
    units = (n_ctx // 2 + 1) * n_sub
    return pl.pallas_call(
        functools.partial(kernel, n_ctx, n_sub),
        out_shape=jax.ShapeDtypeStruct((rows, heads * HEAD_DIM), jnp.bfloat16),
        in_specs=[pl.BlockSpec(memory_space=pltpu.HBM)] * 6,
        out_specs=pl.BlockSpec(memory_space=pltpu.VMEM),
        scratch_shapes=[
            pltpu.VMEM((heads * rows, HEAD_DIM), jnp.bfloat16),
            pltpu.VMEM((units * unit, cols), jnp.bfloat16),
            pltpu.VMEM((units * unit, cols), jnp.bfloat16),
            pltpu.SMEM(doc_lengths.shape, jnp.int32),
            pltpu.VMEM((1, heads * rows), jnp.float32),
            pltpu.VMEM((1, heads * rows), jnp.float32),
            pltpu.VMEM((HEAD_DIM, heads * rows), jnp.float32),
            pltpu.VMEM((rows, heads * rows), jnp.bfloat16),
            pltpu.SemaphoreType.DMA((heads,)),
            pltpu.SemaphoreType.DMA,
            pltpu.SemaphoreType.DMA((2,)),
            pltpu.SemaphoreType.DMA((max(n_sub - 1, 1), 2)),
            pltpu.SemaphoreType.DMA((n_sub, 2)),
            pltpu.SemaphoreType.DMA((per_cache, n_sub, 2)),
            pltpu.SemaphoreType.DMA((units, 2)),
            pltpu.SemaphoreType.DMA((units, 2)),
            pltpu.SemaphoreType.REGULAR,
        ],
        compiler_params=pltpu.CompilerParams(collective_id=0, has_side_effects=True, vmem_limit_bytes=16 * 1024 * 1024),
        name="attend",
    )(
        *(
            pltpu.with_memory_space_constraint(array, pltpu.HBM)
            for array in (
                queries,
                stretch_keys,
                stretch_values,
                cache_keys,
                cache_values,
                doc_lengths,
            )
        )
    )


def solution(mesh):
    in_specs = (
        P(("grp", "ctx"), "head"),
        P(("grp", "ctx", "sub"), "head"),
        P(("grp", "ctx", "sub"), "head"),
        P(("grp", "ctx", "sub"), "head"),
        P(("grp", "ctx", "sub"), "head"),
        P("grp"),
    )
    out_specs = P(("grp", "ctx"), ("head", "sub"))
    return jax.shard_map(
        on_device, mesh=mesh, in_specs=in_specs, out_specs=out_specs, check_vma=False
    )
```

profile of v0, /device:TPU:0, one launch (start us, length us, event | category | flops | bytes accessed | tf_op | source)
XLA Modules:
  0.0 13.7 jit_solution(12520370995752291776)
XLA Ops:
  0.0 12.9 %attend.1 = bf16[128,2048]{1,0:T(8,128)(2,1)S(1)} custom-call(bf16[128,4096]{1,0:T(8,128)(2,1)} %q_hbm.1, bf16[64,512]{1,0:T(8,128)(2,1)} %sk_hbm.1, bf16[64,512]{1,0:T(8,128)(2,1)} %sv_hbm.1, bf16[192,512]{1,0:T(8,128)(2,1)} %ck_hbm.1, bf16[192,512]{1,0:T(8,128)(2,1)} %cv_hbm.1, s32[12]{0:T(128)} %docs_hbm.1), custom_call_target="tpu_custom_call" | custom-call | tf_op jit(solution)/shard_map/attend/pallas_call | solution.py:407
  12.9 0.8 %copy.8 = bf16[128,2048]{1,0:T(8,128)(2,1)} copy(bf16[128,2048]{1,0:T(8,128)(2,1)S(1)} %attend.1) | data formatting | bytes 1048576
where the time goes:
time: 13.8 us; the launch traced here: 13.7 us
  Pallas kernels  12.9 us (93%)
  local copies, waits for them, and re-layouts  0.8 us (6%)
    pallas_call x1, Pallas kernels, on_device(): pl.pallas_call(functools.partial(kernel, n_ctx, n_sub), out_shape=jax.Sha...  12.9 us
    unnamed x1, local copies, waits for them, and re-layouts  0.8 us

commit v1 on v0

--- a/solution.py
+++ b/solution.py
@@ -34,14 +34,14 @@
     docs_sem,
     own_sem,
     pair_send,
-    next_send,
     cache_send,
     relay_send,
     recv_sem,
-    turn_sem,
+    pair_sem,
 ):
     ctx = lax.axis_index("ctx")
     sub = lax.axis_index("sub")
+    other = n_sub - 1 - sub
     flat = ctx * n_sub + sub
     rows = q_hbm.shape[0]
     unit = sk_hbm.shape[0]
@@ -93,19 +93,16 @@
             device_id_type=pl.DeviceIdType.MESH,
         )
 
+    first_owner = (prefix_units - back) // (per_cache * n_sub)
+
     @pl.when(ctx == 0)
     def _():
-        for k in range(back):
-            source = (prefix_units - back + k) // per_cache
-            greet(source // n_sub, source % n_sub)
+        for source in range(first_owner, n_ctx):
+            greet(source, sub)
 
     @pl.when(ctx >= 1)
     def _():
-        for t in range(n_sub):
-            greet(ctx - 1, t)
-
-    for other in range(1, n_sub):
-        greet(ctx, (sub + other) % n_sub)
+        greet(ctx - 1, sub)
 
     docs_copy = pltpu.make_async_copy(docs_hbm, docs, docs_sem)
     docs_copy.start()
@@ -132,119 +129,100 @@
     def offset(j):
         return flat * per_cache + j - (prefix_units - back)
 
-    expected = n_sub - 1 + jnp.where(ctx + 1 < n_ctx, n_sub, 0)
+    expected = (
+        jnp.where(ctx + 1 < n_ctx, 1, 0)
+        + jnp.where(ctx >= first_owner, 1, 0)
+        + jnp.where(sub == 0, 1, 0)
+    )
+    pl.semaphore_wait(barrier, expected)
+
+    @pl.when(sub == 1)
+    def _():
+        greet(ctx, 0)
+
+    @pl.when(sub == 0)
+    def _():
+        pl.semaphore_signal(
+            pair_sem,
+            inc=1,
+            device_id={"ctx": ctx, "sub": 1},
+            device_id_type=pl.DeviceIdType.MESH,
+        )
+
+    def cache_copy(j, t, i):
+        to_slot = offset(j)
+        return remote(
+            cache[i].at[pl.ds(j * unit, unit), columns(t)],
+            slot(bufs[i], to_slot),
+            cache_send.at[j, t, i],
+            recv_sem.at[to_slot, i],
+            0,
+            t,
+        )
+
+    def pair_copy(i):
+        return remote(
+            stretch[i].at[:, columns(other)],
+            slot(bufs[i], back + sub),
+            pair_send.at[i],
+            recv_sem.at[back + sub, i],
+            ctx,
+            other,
+        )
+
+    def relays(k, i, act):
+        @pl.when(ctx + 1 < n_ctx)
+        def _():
+            act(
+                remote(
+                    slot(bufs[i], k),
+                    slot(bufs[i], k - n_sub),
+                    relay_send.at[k, i],
+                    recv_sem.at[k - n_sub, i],
+                    ctx + 1,
+                    sub,
+                )
+            )
+
+    def send_cache(j, t):
+        for i in range(2):
+            cache_copy(j, t, i).start()
+
+    @pl.when(sub == 1)
+    def _():
+        for j in reversed(range(per_cache)):
+
+            @pl.when(offset(j) >= n_sub)
+            def _(j=j):
+                send_cache(j, 1)
+
+    for i in range(2):
+        own_copies[i].wait()
+        relays(back + sub, i, lambda copy: copy.start())
+
+    @pl.when(sub == 1)
+    def _():
+        pl.semaphore_wait(pair_sem, 1)
+
     for j in range(per_cache):
-        expected = expected + jnp.where(offset(j) >= 0, n_sub, 0)
-    pl.semaphore_wait(barrier, expected)
-
-    def cache_copies(j, subs=range(n_sub)):
-        to_slot = offset(j)
-        copies = []
-        for i in range(2):
-            for t in subs:
-                copies.append(
-                    remote(
-                        cache[i].at[pl.ds(j * unit, unit), columns(t)],
-                        slot(bufs[i], to_slot),
-                        cache_send.at[j, t, i],
-                        recv_sem.at[to_slot, i],
-                        0,
-                        t,
-                    )
-                )
-        return copies
-
-    def next_copies():
-        copies = []
-        for t in range(n_sub):
-            for i in range(2):
-                to_slot = back - n_sub + sub
-                copies.append(
-                    remote(
-                        stretch[i].at[:, columns(t)],
-                        slot(bufs[i], to_slot),
-                        next_send.at[t, i],
-                        recv_sem.at[to_slot, i],
-                        ctx + 1,
-                        t,
-                    )
-                )
-        return copies
-
-    def pair_copies():
-        copies = []
-        for other in range(1, n_sub):
-            to_sub = (sub + other) % n_sub
-            for i in range(2):
-                copies.append(
-                    remote(
-                        stretch[i].at[:, columns(to_sub)],
-                        slot(bufs[i], back + sub),
-                        pair_send.at[other - 1, i],
-                        recv_sem.at[back + sub, i],
-                        ctx,
-                        to_sub,
-                    )
-                )
-        return copies
-
-    lowest = (prefix_units - back) // per_cache
-    holder = (prefix_units - back + n_sub) // per_cache
-    gated = lowest != holder and lowest // n_sub == holder // n_sub
-
-    for j in reversed(range(per_cache)):
-
-        @pl.when(offset(j) >= int(gated))
+
+        @pl.when(offset(j) >= n_sub)
         def _(j=j):
-            for copy in cache_copies(j):
-                copy.start()
-
-    @pl.when(ctx + 1 < n_ctx)
-    def _():
-        for copy in next_copies():
-            copy.start()
-
-    for copy in pair_copies():
-        copy.start()
-
-    half = n_sub // 2
-    if gated:
-        for j in range(per_cache):
-
-            @pl.when(offset(j) == n_sub)
-            def _(j=j):
-                for copy in cache_copies(j, range(half)):
-                    copy.wait_send()
-                pl.semaphore_signal(
-                    turn_sem,
-                    inc=1,
-                    device_id={"ctx": ctx, "sub": lowest % n_sub},
-                    device_id_type=pl.DeviceIdType.MESH,
-                )
-
-        for j in range(per_cache):
-
-            @pl.when(offset(j) == 0)
-            def _(j=j):
-                pl.semaphore_wait(turn_sem, 1)
-                for copy in cache_copies(j):
-                    copy.start()
-
-    def relays(k, i, act):
-        if k >= n_sub:
-
-            @pl.when(ctx + 1 < n_ctx)
+            send_cache(j, 0)
+
+            @pl.when(sub == 0)
             def _():
-                act(
-                    remote(
-                        slot(bufs[i], k),
-                        slot(bufs[i], k - n_sub),
-                        relay_send.at[k, i],
-                        recv_sem.at[k - n_sub, i],
-                        ctx + 1,
-                        sub,
-                    )
-                )
+                send_cache(j, 1)
+
+    for j in range(per_cache):
+
+        @pl.when((offset(j) >= 0) & (offset(j) < n_sub))
+        def _(j=j):
+            for t in range(n_sub):
+                send_cache(j, t)
+
+    for i in range(2):
+        pair_copy(i).start()
 
     def arrived(k, i):
         piece = slot(bufs[i], k)
@@ -341,25 +319,21 @@
             here = pl.ds(at, span)
             add(g, at, part_v[:, here], sum_v[:, here], None)
 
-    for copy in own_copies:
-        copy.wait()
+    for i in range(2):
+        arrived(back + other, i)
+        relays(back + other, i, lambda copy: copy.start())
     for copy in q_copies:
         copy.wait()
-    for r in range(n_sub):
-
-        @pl.when(sub != r)
-        def _(r=r):
-            for i in range(2):
-                arrived(back + r, i)
 
     attend(0)
 
     def take(distance, kinds=(0, 1)):
-        for r in reversed(range(n_sub)):
+        for r in (sub, other):
             k = back - distance * n_sub + r
             for i in kinds:
                 arrived(k, i)
-                relays(k, i, lambda copy: copy.start())
+                if distance < reach:
+                    relays(k, i, lambda copy: copy.start())
 
     for distance in range(1, reach + 1):
         if distance < reach:
@@ -370,27 +344,13 @@
 
         @pl.when(offset(j) >= 0)
         def _(j=j):
-            if gated:
-
-                @pl.when(offset(j) != n_sub)
-                def _():
-                    for copy in cache_copies(j, range(half)):
-                        copy.wait_send()
-
-                for copy in cache_copies(j, range(half, n_sub)):
-                    copy.wait_send()
-            else:
-                for copy in cache_copies(j):
-                    copy.wait_send()
-
-    @pl.when(ctx + 1 < n_ctx)
-    def _():
-        for copy in next_copies():
-            copy.wait_send()
-
-    for copy in pair_copies():
-        copy.wait_send()
-    for k in range(back):
+            for t in range(n_sub):
+                for i in range(2):
+                    cache_copy(j, t, i).wait_send()
+
+    for i in range(2):
+        pair_copy(i).wait_send()
+    for k in range(n_sub, back + n_sub):
         for i in range(2):
             relays(k, i, lambda copy: copy.wait_send())
 
@@ -421,8 +381,7 @@
             pltpu.SemaphoreType.DMA((heads,)),
             pltpu.SemaphoreType.DMA,
             pltpu.SemaphoreType.DMA((2,)),
-            pltpu.SemaphoreType.DMA((max(n_sub - 1, 1), 2)),
-            pltpu.SemaphoreType.DMA((n_sub, 2)),
+            pltpu.SemaphoreType.DMA((2,)),
             pltpu.SemaphoreType.DMA((per_cache, n_sub, 2)),
             pltpu.SemaphoreType.DMA((units, 2)),
             pltpu.SemaphoreType.DMA((units, 2)),

time: 13.8 us -> 13.1 us (0.949)
  the two profiles are of different devices: /device:TPU:0 before, /device:TPU:1 now
where the time goes in v1:
time: 13.1 us; the launch traced here: 12.9 us
  Pallas kernels  12.1 us (92%)
  local copies, waits for them, and re-layouts  0.8 us (6%)
    pallas_call x1, Pallas kernels, on_device(): pl.pallas_call(functools.partial(kernel, n_ctx, n_sub), out_shape=jax.Sha...  12.1 us
    unnamed x1, local copies, waits for them, and re-layouts  0.8 us

profile of v1, /device:TPU:1, one launch (start us, length us, event | category | flops | bytes accessed | tf_op | source)
XLA Modules:
  0.0 12.9 jit_solution(11510417864251476392)
XLA Ops:
  0.0 12.1 %attend.1 = bf16[128,2048]{1,0:T(8,128)(2,1)S(1)} custom-call(bf16[128,4096]{1,0:T(8,128)(2,1)} %q_hbm.1, bf16[64,512]{1,0:T(8,128)(2,1)} %sk_hbm.1, bf16[64,512]{1,0:T(8,128)(2,1)} %sv_hbm.1, bf16[192,512]{1,0:T(8,128)(2,1)} %ck_hbm.1, bf16[192,512]{1,0:T(8,128)(2,1)} %cv_hbm.1, s32[12]{0:T(128)} %docs_hbm.1), custom_call_target="tpu_custom_call" | custom-call | tf_op jit(solution)/shard_map/attend/pallas_call | solution.py:367
  12.1 0.8 %copy.8 = bf16[128,2048]{1,0:T(8,128)(2,1)} copy(bf16[128,2048]{1,0:T(8,128)(2,1)S(1)} %attend.1) | data formatting | bytes 1048576

commit v2 on v1

--- a/solution.py
+++ b/solution.py
@@ -30,6 +30,7 @@
     sum_v,
     acc_v,
     part_v,
+    done_v,
     q_sem,
     docs_sem,
     own_sem,
@@ -105,26 +106,32 @@
         greet(ctx - 1, sub)
 
     docs_copy = pltpu.make_async_copy(docs_hbm, docs, docs_sem)
-    docs_copy.start()
     q_copies = []
     for h in range(heads):
         at = pl.multiple_of((sub * heads + h) * HEAD_DIM, HEAD_DIM)
-        copy = pltpu.make_async_copy(
-            q_hbm.at[:, pl.ds(at, HEAD_DIM)],
-            q_v.at[pl.ds(h * rows, rows), :],
-            q_sem.at[h],
-        )
-        copy.start()
-        q_copies.append(copy)
-    own_copies = []
-    for i in range(2):
-        copy = pltpu.make_async_copy(
+        q_copies.append(
+            pltpu.make_async_copy(
+                q_hbm.at[:, pl.ds(at, HEAD_DIM)],
+                q_v.at[pl.ds(h * rows, rows), :],
+                q_sem.at[h],
+            )
+        )
+    own_copies = [
+        pltpu.make_async_copy(
             stretch[i].at[:, columns(sub)],
             slot(bufs[i], back + sub),
             own_sem.at[i],
         )
-        copy.start()
-        own_copies.append(copy)
+        for i in range(2)
+    ]
+
+    def fetch():
+        for copy in [*own_copies, docs_copy, *q_copies]:
+            copy.start()
+
+    @pl.when(ctx < first_owner)
+    def _():
+        fetch()
 
     def offset(j):
         return flat * per_cache + j - (prefix_units - back)
@@ -195,6 +202,10 @@
             @pl.when(offset(j) >= n_sub)
             def _(j=j):
                 send_cache(j, 1)
+
+    @pl.when(ctx >= first_owner)
+    def _():
+        fetch()
 
     for i in range(2):
         own_copies[i].wait()
@@ -279,28 +290,21 @@
                 total = total + sum_v[:, here] * shrink
             if distance < reach:
                 max_v[:, here] = top
-            return weights.astype(jnp.bfloat16), total, shrink
+            return weights, total, shrink
 
         def add(g, at, weights, total, shrink):
             here = pl.ds(at, span)
             values = v_buf[pl.ds(base, rows), pl.ds(g * HEAD_DIM, HEAD_DIM)]
             update = lax.dot_general(
                 values,
-                weights,
+                weights.astype(jnp.bfloat16),
                 (((0,), (0,)), ((), ())),
                 preferred_element_type=jnp.float32,
             )
-            if 0 < distance < reach:
+            if distance > 0:
                 update = update + acc_v[:, here] * shrink
-            if distance < reach:
-                sum_v[:, here] = total
-                acc_v[:, here] = update
-            else:
-                result = (acc_v[:, here] + update * total).astype(out_ref.dtype)
-                for w in range(wide):
-                    piece = result[:, w * rows : (w + 1) * rows]
-                    out_at = (at // rows + w) * HEAD_DIM
-                    out_ref[:, pl.ds(out_at, HEAD_DIM)] = piece.T
+            sum_v[:, here] = total
+            acc_v[:, here] = update
 
         if distance < reach:
             for g, at in blocks:
@@ -309,15 +313,28 @@
         take(distance, (0,))
         for g, at in blocks:
             weights, total, shrink = weigh(g, at)
-            here = pl.ds(at, span)
-            part_v[:, here] = weights
             inverse = 1.0 / total
-            sum_v[:, here] = inverse
-            acc_v[:, here] = acc_v[:, here] * (shrink * inverse)
+            weights = (weights * inverse).astype(jnp.bfloat16)
+            before = acc_v[:, pl.ds(at, span)] * (shrink * inverse)
+            for w in range(wide):
+                here = slice(w * rows, (w + 1) * rows)
+                there = pl.ds(at + w * rows, rows)
+                part_v[there, :] = weights[:, here].T
+                done_v[there, :] = before[:, here].T
         take(distance, (1,))
         for g, at in blocks:
             here = pl.ds(at, span)
-            add(g, at, part_v[:, here], sum_v[:, here], None)
+            values = v_buf[pl.ds(base, rows), pl.ds(g * HEAD_DIM, HEAD_DIM)]
+            update = lax.dot_general(
+                part_v[here, :],
+                values,
+                (((1,), (0,)), ((), ())),
+                preferred_element_type=jnp.float32,
+            )
+            result = (done_v[here, :] + update).astype(out_ref.dtype)
+            for w in range(wide):
+                out_at = (at // rows + w) * HEAD_DIM
+                out_ref[:, pl.ds(out_at, HEAD_DIM)] = result[w * rows : (w + 1) * rows]
 
     for i in range(2):
         arrived(back + other, i)
@@ -377,7 +394,8 @@
             pltpu.VMEM((1, heads * rows), jnp.float32),
             pltpu.VMEM((1, heads * rows), jnp.float32),
             pltpu.VMEM((HEAD_DIM, heads * rows), jnp.float32),
-            pltpu.VMEM((rows, heads * rows), jnp.bfloat16),
+            pltpu.VMEM((heads * rows, rows), jnp.bfloat16),
+            pltpu.VMEM((heads * rows, HEAD_DIM), jnp.float32),
             pltpu.SemaphoreType.DMA((heads,)),
             pltpu.SemaphoreType.DMA,
             pltpu.SemaphoreType.DMA((2,)),

time: 13.1 us -> 13.2 us (level)
  Pallas kernels: 12.1 us -> 12.3 us
    pallas_call x1, Pallas kernels: 12.1 us -> 12.3 us  [on_device(): pl.pallas_call(functools.partial(kernel, n_ctx, n_sub), out_shape=jax.Sha...]
where the time goes in v2:
time: 13.2 us; the launch traced here: 13.1 us
  Pallas kernels  12.3 us (93%)
  local copies, waits for them, and re-layouts  0.8 us (6%)
    pallas_call x1, Pallas kernels, on_device(): pl.pallas_call(functools.partial(kernel, n_ctx, n_sub), out_shape=jax.Sha...  12.3 us
    unnamed x1, local copies, waits for them, and re-layouts  0.8 us

profile of v2, /device:TPU:1, one launch (start us, length us, event | category | flops | bytes accessed | tf_op | source)
XLA Modules:
  0.0 13.1 jit_solution(2854886704914883856)
XLA Ops:
  0.0 12.3 %attend.1 = bf16[128,2048]{1,0:T(8,128)(2,1)S(1)} custom-call(bf16[128,4096]{1,0:T(8,128)(2,1)} %q_hbm.1, bf16[64,512]{1,0:T(8,128)(2,1)} %sk_hbm.1, bf16[64,512]{1,0:T(8,128)(2,1)} %sv_hbm.1, bf16[192,512]{1,0:T(8,128)(2,1)} %ck_hbm.1, bf16[192,512]{1,0:T(8,128)(2,1)} %cv_hbm.1, s32[12]{0:T(128)} %docs_hbm.1), custom_call_target="tpu_custom_call" | custom-call | tf_op jit(solution)/shard_map/attend/pallas_call | solution.py:384
  12.3 0.8 %copy.8 = bf16[128,2048]{1,0:T(8,128)(2,1)} copy(bf16[128,2048]{1,0:T(8,128)(2,1)S(1)} %attend.1) | data formatting | bytes 1048576

commit v3 on v1

--- a/solution.py
+++ b/solution.py
@@ -105,26 +105,32 @@
         greet(ctx - 1, sub)
 
     docs_copy = pltpu.make_async_copy(docs_hbm, docs, docs_sem)
-    docs_copy.start()
     q_copies = []
     for h in range(heads):
         at = pl.multiple_of((sub * heads + h) * HEAD_DIM, HEAD_DIM)
-        copy = pltpu.make_async_copy(
-            q_hbm.at[:, pl.ds(at, HEAD_DIM)],
-            q_v.at[pl.ds(h * rows, rows), :],
-            q_sem.at[h],
-        )
-        copy.start()
-        q_copies.append(copy)
-    own_copies = []
-    for i in range(2):
-        copy = pltpu.make_async_copy(
+        q_copies.append(
+            pltpu.make_async_copy(
+                q_hbm.at[:, pl.ds(at, HEAD_DIM)],
+                q_v.at[pl.ds(h * rows, rows), :],
+                q_sem.at[h],
+            )
+        )
+    own_copies = [
+        pltpu.make_async_copy(
             stretch[i].at[:, columns(sub)],
             slot(bufs[i], back + sub),
             own_sem.at[i],
         )
-        copy.start()
-        own_copies.append(copy)
+        for i in range(2)
+    ]
+
+    def fetch():
+        for copy in [*own_copies, docs_copy, *q_copies]:
+            copy.start()
+
+    @pl.when(ctx < first_owner)
+    def _():
+        fetch()
 
     def offset(j):
         return flat * per_cache + j - (prefix_units - back)
@@ -195,6 +201,10 @@
             @pl.when(offset(j) >= n_sub)
             def _(j=j):
                 send_cache(j, 1)
+
+    @pl.when(ctx >= first_owner)
+    def _():
+        fetch()
 
     for i in range(2):
         own_copies[i].wait()

time: 13.1 us -> 13 us (level)
  no operation moved by 1% of the time
where the time goes in v3:
time: 13 us; the launch traced here: 12.9 us
  Pallas kernels  12 us (92%)
  local copies, waits for them, and re-layouts  0.8 us (6%)
    pallas_call x1, Pallas kernels, on_device(): pl.pallas_call(functools.partial(kernel, n_ctx, n_sub), out_shape=jax.Sha...  12 us
    unnamed x1, local copies, waits for them, and re-layouts  0.8 us

profile of v3, /device:TPU:1, one launch (start us, length us, event | category | flops | bytes accessed | tf_op | source)
XLA Modules:
  0.0 12.9 jit_solution(6065459087528044689)
XLA Ops:
  0.0 12.0 %attend.1 = bf16[128,2048]{1,0:T(8,128)(2,1)S(1)} custom-call(bf16[128,4096]{1,0:T(8,128)(2,1)} %q_hbm.1, bf16[64,512]{1,0:T(8,128)(2,1)} %sk_hbm.1, bf16[64,512]{1,0:T(8,128)(2,1)} %sv_hbm.1, bf16[192,512]{1,0:T(8,128)(2,1)} %ck_hbm.1, bf16[192,512]{1,0:T(8,128)(2,1)} %cv_hbm.1, s32[12]{0:T(128)} %docs_hbm.1), custom_call_target="tpu_custom_call" | custom-call | tf_op jit(solution)/shard_map/attend/pallas_call | solution.py:377
  12.1 0.8 %copy.8 = bf16[128,2048]{1,0:T(8,128)(2,1)} copy(bf16[128,2048]{1,0:T(8,128)(2,1)S(1)} %attend.1) | data formatting | bytes 1048576

commit v4 on v3

--- a/solution.py
+++ b/solution.py
@@ -30,11 +30,13 @@
     sum_v,
     acc_v,
     part_v,
+    shrink_v,
     q_sem,
     docs_sem,
     own_sem,
     pair_send,
     cache_send,
+    skip_send,
     relay_send,
     recv_sem,
     pair_sem,
@@ -100,6 +102,11 @@
         for source in range(first_owner, n_ctx):
             greet(source, sub)
 
+    @pl.when(ctx == 1)
+    def _():
+        for source in range(first_owner, n_ctx):
+            greet(source, sub)
+
     @pl.when(ctx >= 1)
     def _():
         greet(ctx - 1, sub)
@@ -137,7 +144,7 @@
 
     expected = (
         jnp.where(ctx + 1 < n_ctx, 1, 0)
-        + jnp.where(ctx >= first_owner, 1, 0)
+        + jnp.where(ctx >= first_owner, 2, 0)
         + jnp.where(sub == 0, 1, 0)
     )
     pl.semaphore_wait(barrier, expected)
@@ -166,6 +173,17 @@
             t,
         )
 
+    def skip_copy(j, t):
+        to_slot = offset(j) - n_sub
+        return remote(
+            cache[1].at[pl.ds(j * unit, unit), columns(t)],
+            slot(v_buf, to_slot),
+            skip_send.at[j, t],
+            recv_sem.at[to_slot, 1],
+            1,
+            t,
+        )
+
     def pair_copy(i):
         return remote(
             stretch[i].at[:, columns(other)],
@@ -176,8 +194,10 @@
             other,
         )
 
-    def relays(k, i, act):
-        @pl.when(ctx + 1 < n_ctx)
+    def relays(k, i, act, cached=False):
+        skips = (ctx == 0) & (cached and i == 1)
+
+        @pl.when((ctx + 1 < n_ctx) & jnp.logical_not(skips))
         def _():
             act(
                 remote(
@@ -198,9 +218,9 @@
     def _():
         for j in reversed(range(per_cache)):
 
-            @pl.when(offset(j) >= n_sub)
+            @pl.when(offset(j) >= 0)
             def _(j=j):
-                send_cache(j, 1)
+                cache_copy(j, 1, 0).start()
 
     @pl.when(ctx >= first_owner)
     def _():
@@ -214,25 +234,28 @@
     def _():
         pl.semaphore_wait(pair_sem, 1)
 
-    for j in range(per_cache):
-
-        @pl.when(offset(j) >= n_sub)
-        def _(j=j):
-            send_cache(j, 0)
-
-            @pl.when(sub == 0)
-            def _():
-                send_cache(j, 1)
-
-    for j in range(per_cache):
-
-        @pl.when((offset(j) >= 0) & (offset(j) < n_sub))
-        def _(j=j):
-            for t in range(n_sub):
-                send_cache(j, t)
+    for i in range(2):
+        for j in (*range(1, per_cache), 0):
+
+            @pl.when(offset(j) >= 0)
+            def _(j=j, i=i):
+                cache_copy(j, 0, i).start()
+
+        for j in reversed(range(per_cache)):
+
+            @pl.when((offset(j) >= 0) & ((sub == 0) | (i == 1)))
+            def _(j=j, i=i):
+                cache_copy(j, 1, i).start()
 
     for i in range(2):
         pair_copy(i).start()
+    for i in range(2):
+        for j in range(per_cache):
+
+            @pl.when(offset(j) >= n_sub)
+            def _(j=j, i=i):
+                skip_copy(j, i).start()
+
 
     def arrived(k, i):
         piece = slot(bufs[i], k)
@@ -249,8 +272,13 @@
     wide = min(2, per_group)
     span = wide * rows
 
-    def attend(distance):
-        base = (reach - distance) * rows
+    blocks = [
+        (g, (g * per_group + b * wide) * rows)
+        for g in range(groups)
+        for b in range(per_group // wide)
+    ]
+
+    def mask(distance):
         k_pos = (
             rows * (ctx - distance)
             + prefix_units * unit
@@ -260,74 +288,80 @@
         if distance == 0:
             allowed = allowed & (k_pos <= q_pos)
         bias = jnp.where(allowed, 0.0, NEG_FILL)
-        bias = jnp.concatenate([bias] * wide, axis=1)
-        blocks = [
-            (g, (g * per_group + b * wide) * rows)
-            for g in range(groups)
-            for b in range(per_group // wide)
-        ]
-
-        def weigh(g, at):
+        return jnp.concatenate([bias] * wide, axis=1)
+
+    def weigh(distance, bias, g, at):
+        here = pl.ds(at, span)
+        keys = k_buf[pl.ds((reach - distance) * rows, rows), pl.ds(g * HEAD_DIM, HEAD_DIM)]
+        scores = lax.dot_general(
+            keys,
+            q_v[here, :],
+            (((1,), (1,)), ((), ())),
+            preferred_element_type=jnp.float32,
+        )
+        scores = scores + bias
+        top = jnp.max(scores, axis=0, keepdims=True)
+        if distance > 0:
+            before = max_v[:, here]
+            top = jnp.maximum(top, before)
+        weights = jnp.exp2((scores - top) * scale)
+        total = jnp.sum(weights, axis=0, keepdims=True)
+        shrink = None
+        if distance > 0:
+            shrink = jnp.exp2((before - top) * scale)
+            total = total + sum_v[:, here] * shrink
+        if distance < reach:
+            max_v[:, here] = top
+            sum_v[:, here] = total
+        return weights.astype(jnp.bfloat16), total, shrink
+
+    def weighted(distance, g, weights):
+        values = v_buf[pl.ds((reach - distance) * rows, rows), pl.ds(g * HEAD_DIM, HEAD_DIM)]
+        return lax.dot_general(
+            values,
+            weights,
+            (((0,), (0,)), ((), ())),
+            preferred_element_type=jnp.float32,
+        )
+
+    def attend(distance):
+        bias = mask(distance)
+        for g, at in blocks:
             here = pl.ds(at, span)
-            keys = k_buf[pl.ds(base, rows), pl.ds(g * HEAD_DIM, HEAD_DIM)]
-            scores = lax.dot_general(
-                keys,
-                q_v[here, :],
-                (((1,), (1,)), ((), ())),
-                preferred_element_type=jnp.float32,
-            )
-            scores = scores + bias
-            top = jnp.max(scores, axis=0, keepdims=True)
+            weights, _, shrink = weigh(distance, bias, g, at)
+            update = weighted(distance, g, weights)
             if distance > 0:
-                before = max_v[:, here]
-                top = jnp.maximum(top, before)
-            weights = jnp.exp2((scores - top) * scale)
-            total = jnp.sum(weights, axis=0, keepdims=True)
-            shrink = None
-            if distance > 0:
-                shrink = jnp.exp2((before - top) * scale)
-                total = total + sum_v[:, here] * shrink
-            if distance < reach:
-                max_v[:, here] = top
-            return weights.astype(jnp.bfloat16), total, shrink
-
-        def add(g, at, weights, total, shrink):
+                update = update + acc_v[:, here] * shrink
+            acc_v[:, here] = update
+
+    def weigh_all(distance):
+        p = distance - (reach - 1)
+        bias = mask(distance)
+        for g, at in blocks:
             here = pl.ds(at, span)
-            values = v_buf[pl.ds(base, rows), pl.ds(g * HEAD_DIM, HEAD_DIM)]
-            update = lax.dot_general(
-                values,
-                weights,
-                (((0,), (0,)), ((), ())),
-                preferred_element_type=jnp.float32,
-            )
-            if 0 < distance < reach:
-                update = update + acc_v[:, here] * shrink
-            if distance < reach:
-                sum_v[:, here] = total
-                acc_v[:, here] = update
+            weights, total, shrink = weigh(distance, bias, g, at)
+            part_v[pl.ds(p * rows, rows), here] = weights
+            if p == 0:
+                shrink_v[0:1, here] = shrink
             else:
-                result = (acc_v[:, here] + update * total).astype(out_ref.dtype)
+                inverse = 1.0 / total
+                sum_v[:, here] = inverse
+                shrink_v[1:2, here] = shrink * inverse
+
+    def add_all(distance):
+        p = distance - (reach - 1)
+        for g, at in blocks:
+            here = pl.ds(at, span)
+            update = weighted(distance, g, part_v[pl.ds(p * rows, rows), here])
+            if p == 0:
+                update = update + acc_v[:, here] * shrink_v[0:1, here]
+                acc_v[:, here] = update * shrink_v[1:2, here]
+            else:
+                result = (acc_v[:, here] + update * sum_v[:, here]).astype(out_ref.dtype)
                 for w in range(wide):
                     piece = result[:, w * rows : (w + 1) * rows]
                     out_at = (at // rows + w) * HEAD_DIM
                     out_ref[:, pl.ds(out_at, HEAD_DIM)] = piece.T
-
-        if distance < reach:
-            for g, at in blocks:
-                add(g, at, *weigh(g, at))
-            return
-        take(distance, (0,))
-        for g, at in blocks:
-            weights, total, shrink = weigh(g, at)
-            here = pl.ds(at, span)
-            part_v[:, here] = weights
-            inverse = 1.0 / total
-            sum_v[:, here] = inverse
-            acc_v[:, here] = acc_v[:, here] * (shrink * inverse)
-        take(distance, (1,))
-        for g, at in blocks:
-            here = pl.ds(at, span)
-            add(g, at, part_v[:, here], sum_v[:, here], None)
 
     for i in range(2):
         arrived(back + other, i)
@@ -343,12 +377,28 @@
             for i in kinds:
                 arrived(k, i)
                 if distance < reach:
-                    relays(k, i, lambda copy: copy.start())
-
-    for distance in range(1, reach + 1):
-        if distance < reach:
-            take(distance)
+                    relays(k, i, lambda copy: copy.start(), True)
+
+    for distance in range(1, reach - 1):
+        take(distance)
         attend(distance)
+    take(reach - 1, (0,))
+
+    @pl.when(ctx > 0)
+    def _():
+        take(reach - 1, (1,))
+
+    weigh_all(reach - 1)
+    take(reach, (0,))
+    weigh_all(reach)
+
+    @pl.when(ctx == 0)
+    def _():
+        take(reach - 1, (1,))
+
+    add_all(reach - 1)
+    take(reach, (1,))
+    add_all(reach)
 
     for j in range(per_cache):
 
@@ -359,10 +409,17 @@
                     cache_copy(j, t, i).wait_send()
 
     for i in range(2):
+        for j in range(per_cache):
+
+            @pl.when(offset(j) >= n_sub)
+            def _(j=j, i=i):
+                skip_copy(j, i).wait_send()
+
+    for i in range(2):
         pair_copy(i).wait_send()
     for k in range(n_sub, back + n_sub):
         for i in range(2):
-            relays(k, i, lambda copy: copy.wait_send())
+            relays(k, i, lambda copy: copy.wait_send(), k < back)
 
 
 def on_device(queries, stretch_keys, stretch_values, cache_keys, cache_values, doc_lengths):
@@ -387,12 +444,14 @@
             pltpu.VMEM((1, heads * rows), jnp.float32),
             pltpu.VMEM((1, heads * rows), jnp.float32),
             pltpu.VMEM((HEAD_DIM, heads * rows), jnp.float32),
-            pltpu.VMEM((rows, heads * rows), jnp.bfloat16),
+            pltpu.VMEM((2 * rows, heads * rows), jnp.bfloat16),
+            pltpu.VMEM((2, heads * rows), jnp.float32),
             pltpu.SemaphoreType.DMA((heads,)),
             pltpu.SemaphoreType.DMA,
             pltpu.SemaphoreType.DMA((2,)),
             pltpu.SemaphoreType.DMA((2,)),
             pltpu.SemaphoreType.DMA((per_cache, n_sub, 2)),
+            pltpu.SemaphoreType.DMA((per_cache, n_sub)),
             pltpu.SemaphoreType.DMA((units, 2)),
             pltpu.SemaphoreType.DMA((units, 2)),
             pltpu.SemaphoreType.REGULAR,

time: 13 us -> 12.9 us (level)
  no operation moved by 1% of the time
where the time goes in v4:
time: 12.9 us; the launch traced here: 12.8 us
  Pallas kernels  12 us (93%)
  local copies, waits for them, and re-layouts  0.8 us (6%)
    pallas_call x1, Pallas kernels, on_device(): pl.pallas_call(functools.partial(kernel, n_ctx, n_sub), out_shape=jax.Sha...  12 us
    unnamed x1, local copies, waits for them, and re-layouts  0.8 us

profile of v4, /device:TPU:1, one launch (start us, length us, event | category | flops | bytes accessed | tf_op | source)
XLA Modules:
  0.0 12.8 jit_solution(13678424280807826270)
XLA Ops:
  0.0 12.0 %attend.1 = bf16[128,2048]{1,0:T(8,128)(2,1)S(1)} custom-call(bf16[128,4096]{1,0:T(8,128)(2,1)} %q_hbm.1, bf16[64,512]{1,0:T(8,128)(2,1)} %sk_hbm.1, bf16[64,512]{1,0:T(8,128)(2,1)} %sv_hbm.1, bf16[192,512]{1,0:T(8,128)(2,1)} %ck_hbm.1, bf16[192,512]{1,0:T(8,128)(2,1)} %cv_hbm.1, s32[12]{0:T(128)} %docs_hbm.1), custom_call_target="tpu_custom_call" | custom-call | tf_op jit(solution)/shard_map/attend/pallas_call | solution.py:434
  12.0 0.8 %copy.8 = bf16[128,2048]{1,0:T(8,128)(2,1)} copy(bf16[128,2048]{1,0:T(8,128)(2,1)S(1)} %attend.1) | data formatting | bytes 1048576
